TPU v7x, 256 devices: a whole 4x4x8 slice. The times are simulated.
256 devices in a mesh: tm: 32 (over y, z), space: 8 (over x, core).
Axes of the slice: x: 4, y: 4, z: 8, core: 2. Of those that a mesh axis runs over, the one named last changes fastest.
Arguments:
- inverse_factor: bfloat16 [2, 32, 4096, 4096], P(None, 'tm', 'space'), may hold values from -1.5 to 1.5, as said below
- tile_mask: int32 [32, 32], replicated, may hold values 0 or 1
- carry_rate: float32 [32, 4096, 2], P('tm', 'space'), may hold values from 0 to 1
- right_side: float32 [32, 4096, 2, 128], P('tm', 'space'), may hold values from -1.5 to 1.5
- arrow_rows: bfloat16 [32, 4096, 2, 512], P('tm', 'space'), may hold values from -0.0625 to 0.0625
- fixed_rhs: float32 [2, 512, 128], P(None, ('tm', 'space')), may hold values from -6 to 6
- tip_factor: bfloat16 [2, 512, 512], replicated, may hold values from -1 to 1, as said below
Outputs:
- solution: float32 [32, 4096, 2, 128], P('tm', 'space')
- fixed_solution: float32 [2, 512, 128], P(None, ('tm', 'space'))
Inputs may be any that keep to these rules, and one draw needn't show every extreme that they name: `tile_mask`: 1 marks a tile that may be nonzero. `inverse_factor`: only entries on or below the diagonal are read. `tip_factor`: only entries on or below the diagonal are read.
All inputs are finite; a program needn't handle non-finite values.
Results may differ from a plain program's by a relative error of at most 0.022.
Values may be sent and summed in bfloat16 or wider, within the bound.
No kernel may reach another device: no remote copies, remote signals or barrier semaphores. Data moves between devices by JAX's collectives and lax.ppermute only.
A program may use at most 320 MiB of HBM per device.

v0:
```python
import jax
import jax.numpy as jnp
from jax import lax
from jax.sharding import PartitionSpec as P

TILE = 128


def carried_in(shard, axis, join, neutral, backward):
    count = lax.axis_size(axis)
    place = lax.axis_index(axis)
    ahead = count - 1 - place if backward else place
    gathered = jax.tree.map(
        lambda a, kind: lax.all_gather(a.astype(kind), axis), shard, (jnp.bfloat16, jnp.bfloat16)
    )
    state = jax.tree.map(lambda a, e: jnp.zeros_like(a) + jnp.asarray(e, a.dtype), shard, neutral)

    def one(turn, state):
        source = count - 1 - turn if backward else turn
        return join(
            state,
            jax.tree.map(
                lambda a, own: lax.dynamic_index_in_dim(a, source, 0, False).astype(own.dtype),
                gathered,
                shard,
            ),
        )

    return lax.fori_loop(0, ahead, one, state)


def combine(earlier, latter):
    rate_new = latter[0] * earlier[0]
    rest = tuple(
        (value_l + latter[0] * value_e for value_l, value_e in zip(latter[1:], earlier[1:]))
    )
    return (rate_new,) + rest


def tile_keep(tile_table, row_start, row_total, col_total):
    tile_count = tile_table.shape[0]
    tile_ids = jnp.arange(tile_count, dtype=jnp.int32)
    row_index = row_start + jnp.arange(row_total, dtype=jnp.int32)
    col_index = jnp.arange(col_total, dtype=jnp.int32)
    row_onehot = (row_index[:, None] // TILE == tile_ids[None, :]).astype(jnp.float32)
    col_onehot = (col_index[:, None] // TILE == tile_ids[None, :]).astype(jnp.float32)
    marked = jnp.dot(jnp.dot(row_onehot, tile_table.astype(jnp.float32)), col_onehot.T)
    return (marked > 0.5) & (row_index[:, None] >= col_index[None, :])


def on_device(inverse_factor, tile_mask, carry_rate, right_side, arrow_rows, fixed_rhs, tip_factor):
    row_count = right_side.shape[1]
    node_total = inverse_factor.shape[3]
    row_start = lax.axis_index("space") * row_count
    tile_table = jnp.maximum(tile_mask, jnp.eye(tile_mask.shape[0], dtype=jnp.int32))
    weights = inverse_factor[:, 0]
    bf_zero = jnp.zeros((), jnp.bfloat16)
    rate_col = carry_rate[0][:, :, None]
    source = right_side[0]
    unit_rate = jnp.ones_like(rate_col)
    earlier_sum = carried_in(
        (rate_col, source), "tm", combine, (unit_rate, jnp.zeros_like(source)), False
    )
    forward = source + rate_col * earlier_sum[1]
    forward_b = forward.astype(jnp.bfloat16)
    row_keep = tile_keep(tile_table, row_start, row_count, node_total)
    masked_rows = jnp.where(row_keep[None], weights, bf_zero)
    block = masked_rows
    inner_rows = jnp.einsum(
        "hrn,nhk->rhk",
        block,
        lax.all_gather(forward_b, "space", axis=0, tiled=True),
        preferred_element_type=jnp.float32,
    ).astype(jnp.bfloat16)
    block = masked_rows
    scaled = lax.psum_scatter(
        jnp.einsum("hrn,rhk->nhk", block, inner_rows, preferred_element_type=jnp.float32).astype(
            jnp.bfloat16
        ),
        "space",
        scatter_dimension=0,
        tiled=True,
    ).astype(jnp.float32)
    arrow_part = arrow_rows[0]
    coupling = jnp.einsum("rhf,rhk->hfk", arrow_part, forward_b, preferred_element_type=jnp.float32)
    share_rows = fixed_rhs.shape[1]
    share_start = lax.axis_index(("tm", "space")) * share_rows
    contrib = -coupling
    own_part = lax.dynamic_slice_in_dim(contrib, share_start, share_rows, 1) + fixed_rhs
    contrib = lax.dynamic_update_slice_in_dim(contrib, own_part, share_start, 1)
    fixed_forward = lax.psum(contrib, ("tm", "space")).astype(jnp.bfloat16)
    fixed_total = tip_factor.shape[1]
    fixed_index = jnp.arange(fixed_total, dtype=jnp.int32)
    lower_tri = fixed_index[:, None] >= fixed_index[None, :]
    tip_lower = jnp.where(lower_tri[None], tip_factor, bf_zero)
    tip_inner = jnp.einsum(
        "hij,hjk->hik", tip_lower, fixed_forward, preferred_element_type=jnp.float32
    ).astype(jnp.bfloat16)
    fixed_solution = jnp.einsum(
        "hij,hik->hjk", tip_lower, tip_inner, preferred_element_type=jnp.float32
    )
    fixed_own = lax.dynamic_slice_in_dim(fixed_solution, share_start, share_rows, 1)
    fixed_b = fixed_solution.astype(jnp.bfloat16)
    carried = scaled - jnp.einsum(
        "rhf,hfk->rhk", arrow_part, fixed_b, preferred_element_type=jnp.float32
    )
    following = carried_in(
        (rate_col, rate_col * carried), "tm", combine, (unit_rate, jnp.zeros_like(carried)), True
    )
    solution = carried + following[1]
    return (solution[None], fixed_own)


def solution(mesh):
    placed = (
        P(None, "tm", "space", None),
        P(),
        P("tm", "space", None),
        P("tm", "space", None, None),
        P("tm", "space", None, None),
        P(None, ("tm", "space"), None),
        P(),
    )
    return jax.shard_map(
        on_device,
        mesh=mesh,
        in_specs=placed,
        out_specs=(P("tm", "space", None, None), P(None, ("tm", "space"), None)),
        check_vma=False,
    )
```

profile of v0, /device:TPU:2, one launch (start us, length us, event | category | flops | bytes accessed | tf_op | source)
XLA Modules:
  0.0 596.0 jit_solution(12626880782622736189)
XLA Ops:
  7.2 1.9 copy.62
  9.2 1.2 copy.34
  11.1 52.1 %all-gather = bf16[32,512,2]{1,2,0:T(2,128)(2,1)S(1)} all-gather(bf16[1,512,2]{1,2,0:T(2,128)(2,1)S(1)} %convert_element_type.103), channel_id=2, replica_groups=mesh['tm'=32,'space'=8] {'tm'}, dimensions={0}, use_global_device_ids=true | all-gather | bytes 67584 | tf_op jit(solution)/shard_map/all_gather | solution.py:14
  63.2 3.3 copy.37
  66.6 46.1 %all-gather.6.cloned.1.call-done = bf16[32,512,2,128]{3,1,2,0:T(8,128)(2,1)} async-done(((bf16[1,512,2,128]{3,1,2,0:T(8,128)(2,1)}), bf16[32,512,2,128]{3,1,2,0:T(8,128)(2,1)}) %all-gather.6.cloned.1.call-update) | async-done | bytes 8388624 | tf_op jit(solution)/shard_map/all_gather | solution.py:14
  114.4 4.2 fusion
  118.6 154.2 %all-gather.8.cloned.1.call-done = bf16[4096,2,128]{0,2,1:T(8,128)(2,1)} async-done(((bf16[512,2,128]{0,2,1:T(8,128)(2,1)}), bf16[4096,2,128]{0,2,1:T(8,128)(2,1)}) %all-gather.8.cloned.1.call-update) | async-done | bytes 2097168 | tf_op jit(solution)/shard_map/all_gather | solution.py:72
  272.7 13.2 %fusion.4 = bf16[4096,2,128]{0,2,1:T(8,128)(2,1)} fusion(bf16[2,1,512,4096]{3,2,1,0:T(8,128)(2,1)} %param.11, pred[512,4096]{1,0:T(8,128)(4,1)} %fusion, bf16[4096,2,128]{0,2,1:T(8,128)(2,1)} %all-gather.8.cloned.1.call-done), kind=kOutput, calls=%fused_computation.12 | convolution fusion | flops 2157051904 | bytes 14680064 | tf_op jit(solution)/shard_map/hrn,rhk->nhk/dot_general | solution.py:77
  286.7 1.1 dynamic_update_slice.3
  287.8 78.9 %all-reduce.1 = bf16[2,512,128]{1,2,0:T(8,128)(2,1)S(1)} all-reduce(f32[2,512,128]{1,2,0:T(8,128)S(1)} %dynamic_update_slice.3), channel_id=1, replica_groups=mesh['tm'=32,'space'=8] {'tm','space'}, use_global_device_ids=true, to_apply=%region_3.4 | all-reduce | flops 131072 | bytes 786432 | tf_op jit(solution)/shard_map/psum | solution.py:91
  366.7 2.3 fusion.9
  369.0 2.1 multiply_convert_fusion
  371.8 102.9 %all-gather.10.cloned.1.call-done = bf16[16384,2,128]{0,2,1:T(8,128)(2,1)} async-done(((bf16[512,2,128]{0,2,1:T(8,128)(2,1)}), bf16[16384,2,128]{0,2,1:T(8,128)(2,1)}) %all-gather.10.cloned.1.call-update) | async-done | bytes 8388624 | tf_op jit(solution)/shard_map/all_gather | solution.py:14
  474.7 21.1 %copy.52 = bf16[16384,2,128]{2,1,0:T(2,128)(2,1)} copy(bf16[16384,2,128]{0,2,1:T(8,128)(2,1)} %all-gather.10.cloned.1.call-done) | data formatting | bytes 16777216 | tf_op jit(solution)/shard_map/while | solution.py:29
  495.9 92.2 %while.27 = (s32[]{:T(128)}, f32[512,2,128]{2,1,0:T(2,128)S(1)}, s32[]{:T(128)}, bf16[32,512,2,128]{3,2,1,0:T(2,128)(2,1)}, bf16[32,512,2,1]{2,1,3,0:T(8,128)(2,...) while((s32[]{:T(128)}, f32[512,2,128]{2,1,0:T(2,128)S(1)}, s32[]{:T(128)}, ...), condition=%wide.region_5.6_spmd, body=%wide.region_4.5_spmd.sunk | while | flops 394246 | bytes 1321107 | solution.py:29
  495.9 0.9 bitcast_convert_fusion.5
  496.9 2.0 convert_add_fusion.5
  499.8 2.0 convert_add_fusion.5
  502.8 2.0 convert_add_fusion.5
  505.8 2.0 convert_add_fusion.5
  508.8 2.0 convert_add_fusion.5
  511.7 2.0 convert_add_fusion.5
  514.7 2.0 convert_add_fusion.5
  517.7 2.0 convert_add_fusion.5
  520.7 2.0 convert_add_fusion.5
  523.6 2.0 convert_add_fusion.5
  526.6 2.0 convert_add_fusion.5
  529.6 2.0 convert_add_fusion.5
  532.6 2.0 convert_add_fusion.5
  535.5 2.0 convert_add_fusion.5
  538.5 2.0 convert_add_fusion.5
  541.5 2.0 convert_add_fusion.5
  544.5 2.0 convert_add_fusion.5
  547.4 2.0 convert_add_fusion.5
  550.4 2.0 convert_add_fusion.5
  553.4 2.0 convert_add_fusion.5
  556.3 2.0 convert_add_fusion.5
  559.3 2.0 convert_add_fusion.5
  562.3 2.0 convert_add_fusion.5
  565.3 2.0 convert_add_fusion.5
  568.2 2.0 convert_add_fusion.5
  571.2 2.0 convert_add_fusion.5
  574.2 2.0 convert_add_fusion.5
  577.2 2.0 convert_add_fusion.5
  580.1 2.0 convert_add_fusion.5
  583.1 2.0 convert_add_fusion.5
  586.1 2.0 convert_add_fusion.5
  588.4 1.0 copy.48
  (64 shorter events, 32.1 us)
Async XLA Ops:
  7.2 279.1 %copy-start = (bf16[1,512,2,512]{3,2,1,0:T(2,128)(2,1)S(1)}, bf16[1,512,2,512]{3,2,1,0:T(2,128)(2,1)}, u32[]{:S(2)}) copy-start(bf16[1,512,2,512]{3,2,1,0:T(2,128)(2,1)} %param.15) | copy-start | bytes 3145732
  7.2 105.5 %all-gather.6.cloned.1.call-start = ((), (), s32[]{:S(2)}) async-start(), calls=%async_computation.1 | async-start | bytes 8650752 | tf_op jit(solution)/shard_map/all_gather | solution.py:14
  9.1 263.6 %all-gather.8.cloned.1.call-start = ((), (), s32[]{:S(2)}) async-start(), calls=%async_computation.2 | async-start | bytes 2359296 | tf_op jit(solution)/shard_map/all_gather | solution.py:72
  112.8 0.7 copy-start.2
  112.8 1.6 copy-start.4
  114.3 254.7 %reduce-scatter.2.cloned.1.call-start = ((), (), s32[]{:S(2)}) async-start(), calls=%async_computation.3 | async-start | bytes 2359296 | tf_op jit(solution)/shard_map/reduce_scatter | solution.py:76
  118.6 167.5 %copy-start.3 = (f32[2,2,128]{2,1,0:T(2,128)S(1)}, f32[2,2,128]{2,1,0:T(2,128)}, u32[]{:S(2)}) copy-start(f32[2,2,128]{2,1,0:T(2,128)} %param.16) | copy-start | bytes 6148
  118.6 167.7 %copy-start.1 = (bf16[512,2,128]{0,2,1:T(8,128)(2,1)S(1)}, bf16[512,2,128]{0,2,1:T(8,128)(2,1)}, u32[]{:S(2)}) copy-start(bf16[512,2,128]{0,2,1:T(8,128)(2,1)} %fusion.19) | copy-start | bytes 786436
  286.0 188.7 %all-gather.10.cloned.1.call-start = ((), (), s32[]{:S(2)}) async-start(), calls=%async_computation.4 | async-start | bytes 8650752 | tf_op jit(solution)/shard_map/all_gather | solution.py:14
Sparse Core Ops, SparseCore 0:
  11.2 101.4 all-gather.5
  115.0 157.6 all-gather.7
  286.1 34.6 reduce-scatter.1
  371.3 103.2 all-gather.9
where the time goes:
time: 598 us; the launch traced here: 596 us
  waiting for transfers between devices  303 us (51%)
  blocking collectives  131 us (22%)
  other arithmetic  92.9 us (16%)
  local copies, waits for them, and re-layouts  31.4 us (5%)
  matrix products  22.2 us (4%)
  between operations  14 us (2%)
    all_gather x1, waiting for transfers between devices, on_device(): lax.all_gather(forward_b, 'space', axis=0, tiled=True)  154 us
    all_gather x2, waiting for transfers between devices, carried_in(): lax.all_gather(a.astype(kind), axis)  149 us
    psum x1, blocking collectives, on_device(): fixed_forward = lax.psum(contrib, ('tm', 'space')).astype(jnp.bfloat16)  78.9 us
    add x31, other arithmetic, combine(): value_l + latter[0] * value_e  62.3 us
    all_gather x1, blocking collectives, carried_in(): lax.all_gather(a.astype(kind), axis)  52.1 us
    convert_element_type x31, other arithmetic, one(): lax.dynamic_index_in_dim(a, source, 0, False).astype(own.dtype)  28.8 us
    while x4, local copies, waits for them, and re-layouts, carried_in(): return lax.fori_loop(0, ahead, one, state)  24.8 us
    dot_general x1, matrix products, on_device(): jnp.einsum('hrn,rhk->nhk', block, inner_rows, preferred_element_type=jnp....  13.2 us
  transfers between devices with their start and end apart: 4, of which 3 were waited for; matrix products, arithmetic and copies ran while one was open for 2% of the time, Pallas kernels for 0%

commit v1 on v0

--- a/solution.py
+++ b/solution.py
@@ -4,6 +4,18 @@
 from jax.sharding import PartitionSpec as P
 
 TILE = 128
+
+
+def summed_around(x, axis, dim, term):
+    size, index = (lax.axis_size(axis), lax.axis_index(axis))
+    backward = [(i, (i - 1) % size) for i in range(size)]
+    span = x.shape[dim]
+    held = x
+    subtotal = term(held, index * span)
+    for step in range(1, size):
+        held = lax.ppermute(held, axis, backward)
+        subtotal = subtotal + term(held, (index + step) % size * span)
+    return subtotal
 
 
 def carried_in(shard, axis, join, neutral, backward):
@@ -66,11 +78,16 @@
     row_keep = tile_keep(tile_table, row_start, row_count, node_total)
     masked_rows = jnp.where(row_keep[None], weights, bf_zero)
     block = masked_rows
-    inner_rows = jnp.einsum(
-        "hrn,nhk->rhk",
-        block,
-        lax.all_gather(forward_b, "space", axis=0, tiled=True),
-        preferred_element_type=jnp.float32,
+    inner_rows = summed_around(
+        forward_b,
+        "space",
+        0,
+        lambda own_block, at: jnp.einsum(
+            "hrn,nhk->rhk",
+            lax.dynamic_slice_in_dim(block, at, own_block.shape[0], axis=2),
+            own_block,
+            preferred_element_type=jnp.float32,
+        ),
     ).astype(jnp.bfloat16)
     block = masked_rows
     scaled = lax.psum_scatter(

time: 598 us -> 616 us (1.030)
  waiting for transfers between devices: 303 us -> 157 us
  blocking collectives: 131 us -> 269 us
  starting transfers between devices: 0.16 us -> 13.1 us
  other arithmetic: 92.9 us -> 101 us
    all_gather x1 -> x0, waiting for transfers between devices: 154 us -> none  [on_device(): lax.all_gather(forward_b, 'space', axis=0, tiled=True)]
    psum x1, blocking collectives: 78.9 us -> 217 us  [on_device(): fixed_forward = lax.psum(contrib, ('tm', 'space')).astype(jnp.bfloat16)]
    ppermute x0 -> x7, starting transfers between devices: none -> 13 us  [summed_around(): held = lax.ppermute(held, axis, backward)]
    dot_general x0 -> x7, matrix products: none -> 11.9 us  [on_device(): jnp.einsum('hrn,nhk->rhk', lax.dynamic_slice_in_dim(block, at, own_block....]
    ppermute x0 -> x7, waiting for transfers between devices: none -> 9.17 us  [summed_around(): held = lax.ppermute(held, axis, backward)]
    select_n x0 -> x1, other arithmetic: none -> 8.49 us  [on_device(): masked_rows = jnp.where(row_keep[None], weights, bf_zero)]
    dot_general x1, matrix products: 13.2 us -> 6.72 us  [on_device(): jnp.einsum('hrn,rhk->nhk', block, inner_rows, preferred_element_type=jnp....]
  transfers between devices with their start and end apart: 4 -> 10, of which waited for: 3 -> 7; matrix products, arithmetic and copies ran while one was open for 2% -> 6% of each run, Pallas kernels for 0% -> 0%
where the time goes in v1:
time: 616 us; the launch traced here: 613 us
  blocking collectives  269 us (44%)
  waiting for transfers between devices  157 us (25%)
  other arithmetic  101 us (16%)
  local copies, waits for them, and re-layouts  31.1 us (5%)
  matrix products  27.5 us (4%)
  between operations  14 us (2%)
  starting transfers between devices  13.1 us (2%)
    psum x1, blocking collectives, on_device(): fixed_forward = lax.psum(contrib, ('tm', 'space')).astype(jnp.bfloat16)  217 us
    all_gather x2, waiting for transfers between devices, carried_in(): lax.all_gather(a.astype(kind), axis)  148 us
    add x31, other arithmetic, combine(): value_l + latter[0] * value_e  62.3 us
    all_gather x1, blocking collectives, carried_in(): lax.all_gather(a.astype(kind), axis)  52.1 us
    convert_element_type x31, other arithmetic, one(): lax.dynamic_index_in_dim(a, source, 0, False).astype(own.dtype)  28.7 us
    while x4, local copies, waits for them, and re-layouts, carried_in(): return lax.fori_loop(0, ahead, one, state)  24.9 us
    ppermute x7, starting transfers between devices, summed_around(): held = lax.ppermute(held, axis, backward)  13 us
  transfers between devices with their start and end apart: 10, of which 7 were waited for; matrix products, arithmetic and copies ran while one was open for 6% of the time, Pallas kernels for 0%

profile of v1, /device:TPU:2, one launch (start us, length us, event | category | flops | bytes accessed | tf_op | source)
XLA Modules:
  0.0 613.1 jit_solution(5150134408606604293)
XLA Ops:
  11.1 52.1 %all-gather = bf16[32,512,2]{1,2,0:T(2,128)(2,1)S(1)} all-gather(bf16[1,512,2]{1,2,0:T(2,128)(2,1)S(1)} %convert_element_type.100), channel_id=2, replica_groups=mesh['tm'=32,'space'=8] {'tm'}, dimensions={0}, use_global_device_ids=true | all-gather | bytes 67584 | tf_op jit(solution)/shard_map/all_gather | solution.py:26
  63.2 3.3 copy.37
  66.6 46.1 %all-gather.5.cloned.1.call-done = bf16[32,512,2,128]{3,1,2,0:T(8,128)(2,1)} async-done(((bf16[1,512,2,128]{3,1,2,0:T(8,128)(2,1)}), bf16[32,512,2,128]{3,1,2,0:T(8,128)(2,1)}) %all-gather.5.cloned.1.call-update) | async-done | bytes 8388624 | tf_op jit(solution)/shard_map/all_gather | solution.py:26
  113.2 3.9 collective-permute-done
  117.0 1.9 collective-permute-start.1
  119.0 3.9 collective-permute-done.1
  124.8 4.1 fusion
  130.6 8.5 %bitcast_select_fusion = bf16[2,512,4096]{2,1,0:T(8,128)(2,1)} fusion(bf16[2,1,512,4096]{3,2,1,0:T(8,128)(2,1)} %param.11, pred[512,4096]{1,0:T(8,128)(4,1)} %fusion), kind=kLoop, calls=%fused_computation.6 | loop fusion | flops 4194304 | bytes 18874368 | tf_op jit(solution)/shard_map/jit(_where)/select_n | solution.py:79
  140.8 3.1 collective-permute-start.4
  147.8 2.4 collective-permute-start.5
  159.9 6.7 %fusion.1 = bf16[4096,2,128]{0,2,1:T(8,128)(2,1)} fusion(bf16[2,512,4096]{2,1,0:T(8,128)(2,1)} %bitcast_select_fusion, f32[2,128,512]{2,1,0:T(8,128)S(1)} %convolution_add_fusion.1, bf16[512,2,128]{0,2,1:T(8,128)(2,1)S(1)} %collective-permute-done.6, s32[]{:T(128)S(6)} %select_n.122), kind=kOutput, calls=%fused_computation.10 | convolution fusion | flops 1209270272 | bytes 12320772 | tf_op jit(solution)/shard_map/hrn,rhk->nhk/dot_general | solution.py:94
  168.5 216.5 %all-reduce.1 = bf16[2,512,128]{1,2,0:T(8,128)(2,1)S(1)} all-reduce(f32[2,512,128]{1,2,0:T(8,128)S(1)} %dynamic_update_slice.3), channel_id=1, replica_groups=mesh['tm'=32,'space'=8] {'tm','space'}, use_global_device_ids=true, to_apply=%region_3.4 | all-reduce | flops 131072 | bytes 786432 | tf_op jit(solution)/shard_map/psum | solution.py:108
  385.0 2.3 fusion.4
  387.3 2.1 multiply_convert_fusion
  390.1 101.9 %all-gather.7.cloned.1.call-done = bf16[16384,2,128]{0,2,1:T(8,128)(2,1)} async-done(((bf16[512,2,128]{0,2,1:T(8,128)(2,1)}), bf16[16384,2,128]{0,2,1:T(8,128)(2,1)}) %all-gather.7.cloned.1.call-update) | async-done | bytes 8388624 | tf_op jit(solution)/shard_map/all_gather | solution.py:26
  492.0 21.1 %copy.52 = bf16[16384,2,128]{2,1,0:T(2,128)(2,1)} copy(bf16[16384,2,128]{0,2,1:T(8,128)(2,1)} %all-gather.7.cloned.1.call-done) | data formatting | bytes 16777216 | tf_op jit(solution)/shard_map/while | solution.py:41
  513.2 92.0 %while.27 = (s32[]{:T(128)}, f32[512,2,128]{2,1,0:T(2,128)S(1)}, s32[]{:T(128)}, bf16[32,512,2,128]{3,2,1,0:T(2,128)(2,1)}, bf16[32,512,2,1]{2,1,3,0:T(8,128)(2,...) while((s32[]{:T(128)}, f32[512,2,128]{2,1,0:T(2,128)S(1)}, s32[]{:T(128)}, ...), condition=%wide.region_5.6_spmd, body=%wide.region_4.5_spmd.sunk | while | flops 394246 | bytes 1321115 | solution.py:41
  514.2 2.0 convert_add_fusion.5
  517.1 2.0 convert_add_fusion.5
  520.1 2.0 convert_add_fusion.5
  523.1 2.0 convert_add_fusion.5
  526.0 2.0 convert_add_fusion.5
  529.0 2.0 convert_add_fusion.5
  532.0 2.0 convert_add_fusion.5
  534.9 2.0 convert_add_fusion.5
  537.9 2.0 convert_add_fusion.5
  540.9 2.0 convert_add_fusion.5
  543.9 2.0 convert_add_fusion.5
  546.8 2.0 convert_add_fusion.5
  549.8 2.0 convert_add_fusion.5
  552.8 2.0 convert_add_fusion.5
  555.7 2.0 convert_add_fusion.5
  558.7 2.0 convert_add_fusion.5
  561.7 2.0 convert_add_fusion.5
  564.6 2.0 convert_add_fusion.5
  567.6 2.0 convert_add_fusion.5
  570.6 2.0 convert_add_fusion.5
  573.5 2.0 convert_add_fusion.5
  576.5 2.0 convert_add_fusion.5
  579.5 2.0 convert_add_fusion.5
  582.4 2.0 convert_add_fusion.5
  585.4 2.0 convert_add_fusion.5
  588.4 2.0 convert_add_fusion.5
  591.3 2.0 convert_add_fusion.5
  594.3 2.0 convert_add_fusion.5
  597.3 2.0 convert_add_fusion.5
  600.3 2.0 convert_add_fusion.5
  603.2 2.0 convert_add_fusion.5
  (81 shorter events, 55.8 us)
Async XLA Ops:
  7.2 159.8 %copy-start = (bf16[1,512,2,512]{3,2,1,0:T(2,128)(2,1)S(1)}, bf16[1,512,2,512]{3,2,1,0:T(2,128)(2,1)}, u32[]{:S(2)}) copy-start(bf16[1,512,2,512]{3,2,1,0:T(2,128)(2,1)} %param.15) | copy-start | bytes 3145732
  7.2 105.5 %all-gather.5.cloned.1.call-start = ((), (), s32[]{:S(2)}) async-start(), calls=%async_computation.1 | async-start | bytes 8650752 | tf_op jit(solution)/shard_map/all_gather | solution.py:26
  9.1 378.2 %reduce-scatter.2.cloned.1.call-start = ((), (), s32[]{:S(2)}) async-start(), calls=%async_computation.2 | async-start | bytes 2359296 | tf_op jit(solution)/shard_map/reduce_scatter | solution.py:93
  63.2 49.8 %copy-start.1 = (f32[1,512,2]{1,2,0:T(2,128)S(1)}, f32[1,512,2]{1,2,0:T(2,128)}, u32[]{:S(2)}) copy-start(f32[1,512,2]{1,2,0:T(2,128)} %param.13) | copy-start | bytes 12292
  66.6 58.2 %copy-start.3 = (s32[32,32]{1,0:T(8,128)S(1)}, s32[32,32]{1,0:T(8,128)}, u32[]{:S(2)}) copy-start(s32[32,32]{1,0:T(8,128)} %param.12) | copy-start | bytes 12292
  113.1 3.9 collective-permute-start
  117.0 5.8 collective-permute-start.1
  122.8 6.0 collective-permute-start.2
  128.9 11.9 %collective-permute-start.3 = (bf16[512,2,128]{0,2,1:T(8,128)(2,1)S(1)}, bf16[512,2,128]{0,2,1:T(8,128)(2,1)S(1)}, u32[]{:S(2)}, u32[]{:S(2)}) collective-permute-start(bf16[512,2,128]{0,2,1:T(8,128)(2,1)S(1)} %collective-permute-done.2), channel_id=1, source_target_pairs={{0,7},{1,0},{2,1},{3,2},{4,3},{5,4},{6,5},{7,6},{8,15},{9,8},{10,9... | collective-permute-start | bytes 786440 | tf_op jit(solution)/shard_map/ppermute | solution.py:16
  140.8 7.0 %collective-permute-start.4 = (bf16[512,2,128]{0,2,1:T(8,128)(2,1)S(1)}, bf16[512,2,128]{0,2,1:T(8,128)(2,1)S(1)}, u32[]{:S(2)}, u32[]{:S(2)}) collective-permute-start(bf16[512,2,128]{0,2,1:T(8,128)(2,1)S(1)} %collective-permute-done.3), channel_id=1, source_target_pairs={{0,7},{1,0},{2,1},{3,2},{4,3},{5,4},{6,5},{7,6},{8,15},{9,8},{10,9... | collective-permute-start | bytes 786440 | tf_op jit(solution)/shard_map/ppermute | solution.py:16
  147.8 6.3 %collective-permute-start.5 = (bf16[512,2,128]{0,2,1:T(8,128)(2,1)S(1)}, bf16[512,2,128]{0,2,1:T(8,128)(2,1)S(1)}, u32[]{:S(2)}, u32[]{:S(2)}) collective-permute-start(bf16[512,2,128]{0,2,1:T(8,128)(2,1)S(1)} %collective-permute-done.4), channel_id=1, source_target_pairs={{0,7},{1,0},{2,1},{3,2},{4,3},{5,4},{6,5},{7,6},{8,15},{9,8},{10,9... | collective-permute-start | bytes 786440 | tf_op jit(solution)/shard_map/ppermute | solution.py:16
  154.1 5.8 collective-permute-start.6
  157.7 9.0 %copy-start.2 = (f32[2,2,128]{2,1,0:T(2,128)S(1)}, f32[2,2,128]{2,1,0:T(2,128)}, u32[]{:S(2)}) copy-start(f32[2,2,128]{2,1,0:T(2,128)} %param.16) | copy-start | bytes 6148
  166.7 325.3 %all-gather.7.cloned.1.call-start = ((), (), s32[]{:S(2)}) async-start(), calls=%async_computation.3 | async-start | bytes 8650752 | tf_op jit(solution)/shard_map/all_gather | solution.py:26
Sparse Core Ops, SparseCore 0:
  11.2 101.4 all-gather.4
  166.8 169.4 reduce-scatter.1
  389.6 102.2 all-gather.6
